TPU v7x, 32 devices: a whole 2x2x4 slice. The times are simulated.
32 devices in a mesh: groups: 2 (over y), ctx: 4 (over z), section: 2 (over x), mp: 2 (over core).
Axes of the slice: x: 2, y: 2, z: 4, core: 2. Of those that a mesh axis runs over, the one named last changes fastest.
Arguments:
- spans: bfloat16 [2, 1024, 6144], P('section', ('groups', 'ctx'), 'mp'), parts along dimension 1, may hold values from -6 to 6
- norm_gain: float32 [2, 6144], P('section', 'mp'), may hold values from 0.25 to 1.75
- w_in: bfloat16 [2, 6144, 3, 4096], P('section', 'mp', None, 'ctx'), may hold values from -0.078125 to 0.078125
- filters: bfloat16 [2, 4096, 128], P('section', 'ctx'), may hold values from -0.5 to 0.5
- w_out: bfloat16 [2, 4096, 6144], P('section', 'ctx', 'mp'), may hold values from -0.09375 to 0.09375
- prompt_len: int32 [4], P(('groups', 'section')), parts along dimension 0, may hold values from 128 to 512
- needles: int32 [2, 128], P('section', 'groups'), parts along dimension 1, may hold values from 0 to 511
Outputs:
- advanced: bfloat16 [2, 1024, 6144], P('section', ('groups', 'ctx'), 'mp'), parts along dimension 1
- needle_states: bfloat16 [2, 128, 4096], P('section', 'groups', 'ctx'), parts along dimension 1
There are 2 independent parts, one for each index of `groups`. A program takes and returns all parts, laid end to end along the dimension named above; an argument that names none is the same for every part. Nothing has to cross between parts.
All inputs are finite; a program needn't handle non-finite values.
Results may differ from a plain program's by a relative error of at most 0.02.
Values may be sent and summed in bfloat16 or wider, within the bound.
No kernel may reach another device: no remote copies, remote signals or barrier semaphores. Data moves between devices by JAX's collectives and lax.ppermute only.
A program may use at most 256 MiB of HBM per device.

v0:
```python
import jax
import jax.numpy as jnp
from jax import lax
from jax.sharding import PartitionSpec as P

norm_eps = 1e-06


def shifted(value, axis, steps):
    count = lax.axis_size(axis)
    pairs = [(source, (source + steps) % count) for source in range(count)]
    return lax.ppermute(value, axis, pairs)


def band_conv(mixed, filter_taps):
    span_len, channels = mixed.shape
    tap_count = filter_taps.shape[1]
    row_idx = jnp.arange(tap_count)[:, None]
    col_idx = jnp.arange(tap_count)[None, :]
    offset = row_idx - col_idx
    table = jnp.take(filter_taps, jnp.where(offset >= 0, offset, offset + tap_count), axis=1)
    zero_band = jnp.zeros_like(table)
    near_band = jnp.where((offset >= 0)[None, :, :], table, zero_band)
    far_band = jnp.where((offset < 0)[None, :, :], table, zero_band)
    blocked = mixed.reshape(span_len // tap_count, tap_count, channels)
    previous = jnp.concatenate(
        [jnp.zeros((1, tap_count, channels), mixed.dtype), blocked[:-1]], axis=0
    )
    conv = jnp.einsum("cts,bsc->btc", near_band, blocked, preferred_element_type=jnp.float32)
    conv = conv + jnp.einsum("cts,bsc->btc", far_band, previous, preferred_element_type=jnp.float32)
    return conv.reshape(span_len, channels)


def mix_channels(proj, squares, filter_taps, live, full_width):
    scale = lax.rsqrt(squares / full_width + norm_eps)[:, None]
    query = proj[:, 0] * scale
    mixed = (proj[:, 1] * scale * (proj[:, 2] * scale) * live).astype(jnp.bfloat16)
    conv = band_conv(mixed, filter_taps)
    return (query * conv * live).astype(jnp.bfloat16)


def on_device(spans, norm_gain, w_in, filters, w_out, prompt_len, needles):
    x_local = spans[0]
    gain_local = norm_gain[0]
    w_local = w_in[0]
    half_d = x_local.shape[1]
    channels = w_local.shape[2]
    row_count = x_local.shape[0]
    span_len = row_count * lax.axis_size("ctx")
    full_width = half_d * lax.axis_size("mp")
    w_flat = w_local.reshape(half_d, 3 * channels)
    piece = lax.all_gather(x_local, "ctx", axis=0, tiled=True)
    piece_f = piece.astype(jnp.float32)
    scaled = (piece_f * gain_local[None, :]).astype(jnp.bfloat16)
    part = jnp.dot(scaled, w_flat, preferred_element_type=jnp.float32).reshape(
        piece.shape[0], 3, channels
    )
    squares = jnp.sum(piece_f * piece_f, axis=1)
    square_acc = squares
    positions = jnp.arange(span_len)
    live = (positions < prompt_len[0]).astype(jnp.float32)[:, None]
    proj, squares = (
        lax.psum(part.astype(jnp.bfloat16), "mp").astype(jnp.float32),
        lax.psum(square_acc.astype(jnp.bfloat16), "mp").astype(jnp.float32),
    )
    gated = mix_channels(proj, squares, filters[0], live, full_width)
    w_out_local = w_out[0]
    out = lax.psum_scatter(
        jnp.dot(gated, w_out_local, preferred_element_type=jnp.float32).astype(jnp.bfloat16),
        "ctx",
        scatter_dimension=0,
        tiled=True,
    ).astype(jnp.float32)
    updated = (x_local.astype(jnp.float32) + out).astype(jnp.bfloat16)
    advanced = shifted(updated, "section", 1)[None]
    one_hot = (needles[0][:, None] == positions[None, :]).astype(jnp.bfloat16)
    picked = jnp.dot(one_hot, gated, preferred_element_type=jnp.float32).astype(jnp.bfloat16)[None]
    return (advanced, picked)


def solution(mesh):
    return jax.shard_map(
        on_device,
        mesh=mesh,
        in_specs=(
            P("section", ("groups", "ctx"), "mp"),
            P("section", "mp"),
            P("section", "mp", None, "ctx"),
            P("section", "ctx", None),
            P("section", "ctx", "mp"),
            P(("groups", "section")),
            P("section", "groups"),
        ),
        out_specs=(P("section", ("groups", "ctx"), "mp"), P("section", "groups", "ctx")),
        check_vma=False,
    )
```

profile of v0, /device:TPU:0, one launch (start us, length us, event | category | flops | bytes accessed | tf_op | source)
XLA Modules:
  0.0 371.3 jit_solution(17465330520890966880)
XLA Ops:
  7.2 0.0 all-gather.3.cloned.1.call-start
  7.2 0.7 all-gather.3.cloned.1.call-update
  7.9 0.0 copy-start.8
  7.9 0.0 all-reduce.3.cloned.1.call-start
  8.0 24.8 %copy.16 = bf16[1,3072,3,1024]{1,3,2,0:T(8,128)(2,1)} copy(bf16[1,3072,3,1024]{3,1,2,0:T(8,128)(2,1)} %param.9) | data formatting | bytes 37748736 | tf_op args[2]
  32.7 43.0 %all-gather.3.cloned.1.call-done = bf16[1,512,3072]{2,1,0:T(8,128)(2,1)} async-done(((bf16[1,128,3072]{2,1,0:T(8,128)(2,1)}), bf16[1,512,3072]{2,1,0:T(8,128)(2,1)}) %all-gather.3.cloned.1.call-update) | async-done | bytes 3145744 | tf_op jit(solution)/shard_map/all_gather | solution.py:52
  75.7 0.0 copy-done.8
  75.7 15.9 %fusion.25 = bf16[512,3,1024]{2,0,1:T(8,128)(2,1)} fusion(bf16[1,3072,3,1024]{1,3,2,0:T(8,128)(2,1)} %copy.16, bf16[1,512,3072]{2,1,0:T(8,128)(2,1)} %all-gather.3.cloned.1.call-done, f32[3072]{0:T(1024)S(1)} %bitcast.96), kind=kOutput, calls=%fused_computation.26 | convolution fusion | flops 9669967872 | bytes 25178112 | tf_op jit(solution)/shard_map/dot_general | solution.py:55
  91.7 0.0 copy-start.6
  91.7 0.0 all-reduce.3.cloned.1.call-update
  91.7 0.0 reduce-scatter.2.cloned.1.call-start
  92.4 0.2 copy-done.6
  92.6 0.1 copy.20
  92.8 70.0 %gather_fusion = bf16[16384,1024]{1,0:T(8,128)(2,1)} fusion(bf16[1024,128]{0,1:T(8,128)(2,1)S(1)} %bitcast.86, s32[16384]{0:T(1024)S(1)} %fusion.45), kind=kCustom, calls=%fused_computation | custom fusion | bytes 67174400 | tf_op jit(solution)/shard_map/jit(_take)/gather | solution.py:21
  162.8 46.1 %copy.21 = bf16[128,128,1024]{1,0,2:T(8,128)(2,1)} copy(bf16[128,128,1024]{2,1,0:T(8,128)(2,1)} %bitcast.87) | data formatting | bytes 67108864 | tf_op jit(solution)/shard_map/jit(_take)/gather | solution.py:21
  209.0 0.0 copy-done.3
  209.0 0.7 fusion.15
  209.7 2.6 psum.15
  212.4 0.0 all-reduce.3.cloned.1.call-done
  212.4 4.7 %fusion.59 = (f32[512,1,1024]{2,0,1:T(8,128)}, f32[512,1,1024]{2,0,1:T(8,128)}, f32[512,1,1024]{2,0,1:T(8,128)}) fusion(bf16[512,3,1024]{2,0,1:T(8,128)(2,1)} %all-reduce.3.cloned.1.call-done), kind=kLoop, calls=%fused_computation.74 | loop fusion | bytes 12582912 | tf_op jit(solution)/shard_map/slice | solution.py:36
  217.1 3.1 copy.17
  220.2 0.0 copy-done
  220.2 0.7 convert_element_type.62
  220.9 0.0 copy-start.1
  220.9 0.6 slice_bitcast_fusion.1
  221.5 2.0 copy-done.1
  223.5 0.3 fusion.34
  223.8 0.7 copy.22
  224.6 0.0 copy-start.2
  224.6 3.1 copy.19
  227.7 0.0 copy-done.2
  227.7 1.8 copy.18
  229.5 22.9 %fusion = f32[1024,4,128]{2,1,0:T(4,128)} fusion(pred[128,128]{1,0:T(8,128)(4,1)S(1)} %get-tuple-element.11, bf16[128,128,1024]{1,0,2:T(8,128)(2,1)} %copy.21, pred[128,128]{1,0:T(8,128)(4,1)S(1)} %get-tuple-element.12, bf16[3,128,1024]{1,0,2:T(4,128)(2,1)S(1)} %copy.22), kind=kOutput, calls=%fused_computation.1 | convolution fusion | flops 167772160 | bytes 36470784 | tf_op jit(solution)/shard_map/cts,bsc->btc/dot_general | solution.py:30
  252.4 0.0 copy-done.5
  252.4 23.4 %multiply_convert_fusion = (bf16[4,128,1024]{1,0,2:T(4,128)(2,1)S(1)}, f32[4,128,1024]{1,0,2:T(4,128)}) fusion(f32[4,128,1024]{1,0,2:T(4,128)S(1)} %copy-done.5, f32[4,128]{1,0:T(4,128)S(1)} %fusion.52, f32[4,128]{1,0:T(4,128)S(1)} %get-tuple-element.7, f32[1024,4,128]{2,1,0:T(4,128)} %fusion, pred[128,128]{1,0:T(8,128)(4,1)S(1)} %fusion.48, ...), kind=kOutput, calls=%fused_computation.31 | convolution fusion | flops 173015040 | bytes 45125632 | tf_op jit(solution)/shard_map/cts,bsc->btc/dot_general | solution.py:29
  275.8 7.6 %fusion.18 = bf16[512,3072]{1,0:T(8,128)(2,1)} fusion(bf16[1,1024,3072]{2,1,0:T(8,128)(2,1)} %param.11, bf16[128,8,4,128]{3,2,1,0:T(4,128)(2,1)S(1)} %bitcast.97), kind=kOutput, calls=%fused_computation.22 | convolution fusion | flops 3222798336 | bytes 10485760 | tf_op jit(solution)/shard_map/dot_general | solution.py:69
  283.4 0.0 reduce-scatter.2.cloned.1.call-update
  283.4 59.2 %reduce-scatter.2.cloned.1.call-done = bf16[128,3072]{1,0:T(8,128)(2,1)} async-done(((bf16[512,3072]{1,0:T(8,128)(2,1)}), bf16[128,3072]{1,0:T(8,128)(2,1)}) %reduce-scatter.2.cloned.1.call-update) | async-done | bytes 786448 | tf_op jit(solution)/shard_map/reduce_scatter | solution.py:68
  342.6 0.0 copy-done.4
  342.6 2.2 fusion.35
  344.9 1.5 collective-permute-start
  346.3 1.9 copy.23
  348.3 0.0 copy-start.7
  348.3 2.2 fusion.31
  350.4 0.0 copy-done.7
  350.5 1.0 fusion.38
  351.4 12.5 %collective-permute-done = bf16[128,3072]{1,0:T(8,128)(2,1)S(1)} collective-permute-done((bf16[128,3072]{1,0:T(8,128)(2,1)}, bf16[128,3072]{1,0:T(8,128)(2,1)S(1)}, u32[]{:S(2)}, u32[]{:S(2)}) %collective-permute-start) | collective-permute-done | bytes 786464 | tf_op jit(solution)/shard_map/ppermute | solution.py:12
  363.9 0.9 copy.32
  (10 shorter events, 0.1 us)
Async XLA Ops:
  7.2 68.6 %all-gather.3.cloned.1.call-start = ((), (), s32[]{:S(2)}) async-start(), calls=%async_computation.3 | async-start | bytes 3932160 | tf_op jit(solution)/shard_map/all_gather | solution.py:52
  7.9 67.8 %copy-start.8 = (f32[1,3072]{1,0:T(1,128)S(1)}, f32[1,3072]{1,0:T(1,128)}, u32[]{:S(2)}) copy-start(f32[1,3072]{1,0:T(1,128)} %param.8) | copy-start | bytes 36868
  7.9 204.5 %all-reduce.3.cloned.1.call-start = ((), (), s32[]{:S(2)}) async-start(), calls=%async_computation.1 | async-start | bytes 6291456 | tf_op jit(solution)/shard_map/psum | solution.py:63
  91.7 0.9 copy-start.6
  91.7 250.9 %reduce-scatter.2.cloned.1.call-start = ((), (), s32[]{:S(2)}) async-start(), calls=%async_computation.2 | async-start | bytes 3932160 | tf_op jit(solution)/shard_map/reduce_scatter | solution.py:68
  162.8 46.2 %copy-start.3 = (bf16[1,512,3072]{2,1,0:T(8,128)(2,1)S(1)}, bf16[1,512,3072]{2,1,0:T(8,128)(2,1)}, u32[]{:S(2)}) copy-start(bf16[1,512,3072]{2,1,0:T(8,128)(2,1)} %all-gather.3.cloned.1.call-done) | copy-start | bytes 9437188
  217.1 3.1 copy-start
  220.9 2.6 copy-start.1
  224.6 3.1 copy-start.2
  229.5 22.9 %copy-start.5 = (f32[4,128,1024]{1,0,2:T(4,128)S(1)}, f32[4,128,1024]{1,0,2:T(4,128)}, u32[]{:S(2)}) copy-start(f32[4,128,1024]{1,0,2:T(4,128)} %copy.17) | copy-start | bytes 6291460
  283.4 59.2 %copy-start.4 = (bf16[1,128,3072]{2,1,0:T(8,128)(2,1)S(1)}, bf16[1,128,3072]{2,1,0:T(8,128)(2,1)}, u32[]{:S(2)}) copy-start(bf16[1,128,3072]{2,1,0:T(8,128)(2,1)} %param.7) | copy-start | bytes 2359300
  344.9 19.1 %collective-permute-start = (bf16[128,3072]{1,0:T(8,128)(2,1)}, bf16[128,3072]{1,0:T(8,128)(2,1)S(1)}, u32[]{:S(2)}, u32[]{:S(2)}) collective-permute-start(bf16[128,3072]{1,0:T(8,128)(2,1)} %fusion.35), channel_id=1, source_target_pairs={{0,2},{2,0},{1,3},{3,1},{4,6},{6,4},{5,7},{7,5},{8,10},{10,8},{9,1... | collective-permute-start | bytes 2359304 | tf_op jit(solution)/shard_map/ppermute | solution.py:12
  348.3 2.2 copy-start.7
Sparse Core Ops, SparseCore 0:
  9.5 66.1 all-gather.2
  91.8 21.9 all-reduce.2
  283.6 59.0 reduce-scatter.1
where the time goes:
time: 373 us; the launch traced here: 371 us
  local copies, waits for them, and re-layouts  160 us (43%)
  waiting for transfers between devices  115 us (31%)
  matrix products  70.8 us (19%)
  between operations  14.6 us (4%)
  other arithmetic  6.21 us (2%)
    gather x2, local copies, waits for them, and re-layouts, band_conv(): jnp.take(filter_taps, jnp.where(offset >= 0, offset, offset + tap_count),...  116 us
    reduce_scatter x1, waiting for transfers between devices, on_device(): lax.psum_scatter(jnp.dot(gated, w_out_local, preferred_element_type=jnp.f...  59.2 us
    all_gather x1, waiting for transfers between devices, on_device(): piece = lax.all_gather(x_local, 'ctx', axis=0, tiled=True)  43 us
    unnamed x21, local copies, waits for them, and re-layouts  28 us
    dot_general x1, matrix products, band_conv(): jnp.einsum('cts,bsc->btc', near_band, blocked, preferred_element_type=jnp...  23.4 us
    dot_general x1, matrix products, band_conv(): jnp.einsum('cts,bsc->btc', far_band, previous, preferred_element_type=jnp...  22.9 us
    dot_general x1, matrix products, on_device(): jnp.dot(scaled, w_flat, preferred_element_type=jnp.float32)  15.9 us
    ppermute x1, waiting for transfers between devices, shifted(): return lax.ppermute(value, axis, pairs)  12.5 us
  transfers between devices with their start and end apart: 4, of which 3 were waited for; matrix products, arithmetic and copies ran while one was open for 40% of the time, Pallas kernels for 0%

commit v1 on v0

--- a/solution.py
+++ b/solution.py
@@ -2,6 +2,7 @@
 import jax.numpy as jnp
 from jax import lax
 from jax.sharding import PartitionSpec as P
+from jax.lax import axis_index, axis_size, ppermute
 
 norm_eps = 1e-06
 
@@ -49,7 +50,17 @@
     span_len = row_count * lax.axis_size("ctx")
     full_width = half_d * lax.axis_size("mp")
     w_flat = w_local.reshape(half_d, 3 * channels)
-    piece = lax.all_gather(x_local, "ctx", axis=0, tiled=True)
+    in_order = [x_local]
+    axis_len = axis_size("ctx")
+    dev = 0
+    while dev < axis_len - 1:
+        in_order.append(
+            ppermute(in_order[-1], "ctx", [(idx, (idx + 1) % axis_len) for idx in range(axis_len)])
+        )
+        dev += 1
+    piece = jnp.roll(
+        jnp.concatenate(in_order[::-1], 0), (axis_index("ctx") + 1) * x_local.shape[0], 0
+    )
     piece_f = piece.astype(jnp.float32)
     scaled = (piece_f * gain_local[None, :]).astype(jnp.bfloat16)
     part = jnp.dot(scaled, w_flat, preferred_element_type=jnp.float32).reshape(

time: 373 us -> 382 us (1.024)
  local copies, waits for them, and re-layouts: 160 us -> 164 us
    all_gather x1 -> x0, waiting for transfers between devices: 43 us -> none  [on_device(): piece = lax.all_gather(x_local, 'ctx', axis=0, tiled=True)]
    ppermute x0 -> x3, waiting for transfers between devices: none -> 40.3 us  [on_device(): ppermute(in_order[-1], 'ctx', [(idx, (idx + 1) % axis_len) for idx in ran...]
    unnamed x21 -> x32, local copies, waits for them, and re-layouts: 28 us -> 31.4 us
  transfers between devices with their start and end apart: 4 -> 6, of which waited for: 3 -> 4; matrix products, arithmetic and copies ran while one was open for 40% -> 39% of each run, Pallas kernels for 0% -> 0%
where the time goes in v1:
time: 382 us; the launch traced here: 380 us
  local copies, waits for them, and re-layouts  164 us (43%)
  waiting for transfers between devices  115 us (30%)
  matrix products  70.8 us (19%)
  between operations  14.9 us (4%)
  other arithmetic  8.11 us (2%)
  starting transfers between devices  4.67 us (1%)
    gather x2, local copies, waits for them, and re-layouts, band_conv(): jnp.take(filter_taps, jnp.where(offset >= 0, offset, offset + tap_count),...  116 us
    reduce_scatter x1, waiting for transfers between devices, on_device(): lax.psum_scatter(jnp.dot(gated, w_out_local, preferred_element_type=jnp.f...  61.8 us
    ppermute x3, waiting for transfers between devices, on_device(): ppermute(in_order[-1], 'ctx', [(idx, (idx + 1) % axis_len) for idx in ran...  40.3 us
    unnamed x32, local copies, waits for them, and re-layouts  31.4 us
    dot_general x1, matrix products, band_conv(): jnp.einsum('cts,bsc->btc', near_band, blocked, preferred_element_type=jnp...  23.3 us
    dot_general x1, matrix products, band_conv(): jnp.einsum('cts,bsc->btc', far_band, previous, preferred_element_type=jnp...  22.9 us
    dot_general x1, matrix products, on_device(): jnp.dot(scaled, w_flat, preferred_element_type=jnp.float32)  15.9 us
    ppermute x1, waiting for transfers between devices, shifted(): return lax.ppermute(value, axis, pairs)  12.5 us
  transfers between devices with their start and end apart: 6, of which 4 were waited for; matrix products, arithmetic and copies ran while one was open for 39% of the time, Pallas kernels for 0%

profile of v1, /device:TPU:0, one launch (start us, length us, event | category | flops | bytes accessed | tf_op | source)
XLA Modules:
  0.0 379.7 jit_solution(12340919357047818298)
XLA Ops:
  7.2 0.0 all-reduce.3.cloned.1.call-start
  7.2 3.1 collective-permute-start
  10.3 19.8 %collective-permute-done = bf16[128,3072]{1,0:T(8,128)(2,1)S(1)} collective-permute-done((bf16[128,3072]{1,0:T(8,128)(2,1)}, bf16[128,3072]{1,0:T(8,128)(2,1)S(1)}, u32[]{:S(2)}, u32[]{:S(2)}) %collective-permute-start) | collective-permute-done | bytes 786464 | tf_op jit(solution)/shard_map/ppermute | solution.py:58
  30.1 0.0 collective-permute-start.1
  30.1 20.5 %collective-permute-done.1 = bf16[128,3072]{1,0:T(8,128)(2,1)S(1)} collective-permute-done((bf16[128,3072]{1,0:T(8,128)(2,1)S(1)}, bf16[128,3072]{1,0:T(8,128)(2,1)S(1)}, u32[]{:S(2)}, u32[]{:S(2)}) %collective-permute-start.1) | collective-permute-done | bytes 786464 | tf_op jit(solution)/shard_map/ppermute | solution.py:58
  50.6 0.0 collective-permute-start.2
  50.6 24.7 %copy.16 = bf16[1,3072,3,1024]{1,3,2,0:T(8,128)(2,1)} copy(bf16[1,3072,3,1024]{3,1,2,0:T(8,128)(2,1)} %param.9) | data formatting | bytes 37748736 | tf_op args[2]
  75.3 0.0 collective-permute-done.2
  75.3 0.1 constant_dynamic-update-slice_fusion.7
  75.4 0.1 constant_dynamic-update-slice_fusion.6
  75.5 0.1 constant_dynamic-update-slice_fusion.5
  75.5 0.1 constant_dynamic-update-slice_fusion.4
  75.6 0.1 constant_dynamic-update-slice_fusion.3
  75.6 0.1 constant_dynamic-update-slice_fusion.2
  75.7 0.1 constant_dynamic-update-slice_fusion.1
  75.8 0.1 constant_dynamic-update-slice_fusion
  75.8 2.7 copy-done.5
  78.5 15.9 %fusion.25 = bf16[512,3,1024]{2,0,1:T(8,128)(2,1)} fusion(bf16[1,3072,3,1024]{1,3,2,0:T(8,128)(2,1)} %copy.16, f32[3072]{0:T(1024)S(1)} %bitcast.89, bf16[1024,3072]{1,0:T(8,128)(2,1)} %copy-done.5, s32[]{:T(128)S(6)} %select_n.55), kind=kOutput, calls=%fused_computation.26 | convolution fusion | flops 9669967872 | bytes 25178116 | tf_op jit(solution)/shard_map/dot_general | solution.py:66
  94.4 0.0 all-reduce.3.cloned.1.call-update
  94.5 0.0 reduce-scatter.2.cloned.1.call-start
  95.2 0.1 copy.20
  95.4 69.9 %gather_fusion = bf16[16384,1024]{1,0:T(8,128)(2,1)} fusion(bf16[1024,128]{0,1:T(8,128)(2,1)S(1)} %bitcast.78, s32[16384]{0:T(1024)S(1)} %fusion.44), kind=kCustom, calls=%fused_computation | custom fusion | bytes 67174400 | tf_op jit(solution)/shard_map/jit(_take)/gather | solution.py:22
  165.2 46.0 %copy.21 = bf16[128,128,1024]{1,0,2:T(8,128)(2,1)} copy(bf16[128,128,1024]{2,1,0:T(8,128)(2,1)} %bitcast.79) | data formatting | bytes 67108864 | tf_op jit(solution)/shard_map/jit(_take)/gather | solution.py:22
  211.3 2.6 fusion.15
  213.9 2.6 psum.15
  216.6 0.0 all-reduce.3.cloned.1.call-done
  216.6 4.9 %fusion.59 = (f32[512,1,1024]{2,0,1:T(8,128)}, f32[512,1,1024]{2,0,1:T(8,128)}, f32[512,1,1024]{2,0,1:T(8,128)}) fusion(bf16[512,3,1024]{2,0,1:T(8,128)(2,1)} %all-reduce.3.cloned.1.call-done), kind=kLoop, calls=%fused_computation.82 | loop fusion | bytes 12582912 | tf_op jit(solution)/shard_map/slice | solution.py:37
  221.5 2.9 copy.17
  224.4 0.7 convert_element_type.62
  225.1 2.6 copy-done.1
  227.7 0.6 slice_bitcast_fusion.1
  228.3 0.3 fusion.34
  228.6 1.4 copy.22
  230.1 3.0 copy.19
  233.1 1.8 copy.18
  234.9 22.9 %fusion = f32[1024,4,128]{2,1,0:T(4,128)} fusion(pred[128,128]{1,0:T(8,128)(4,1)S(1)} %get-tuple-element.11, bf16[128,128,1024]{1,0,2:T(8,128)(2,1)} %copy.21, pred[128,128]{1,0:T(8,128)(4,1)S(1)} %get-tuple-element.12, bf16[3,128,1024]{1,0,2:T(4,128)(2,1)S(1)} %copy-done.7), kind=kOutput, calls=%fused_computation.1 | convolution fusion | flops 167772160 | bytes 36470784 | tf_op jit(solution)/shard_map/cts,bsc->btc/dot_general | solution.py:31
  257.8 23.3 %multiply_convert_fusion = (bf16[4,128,1024]{1,0,2:T(4,128)(2,1)S(1)}, f32[4,128,1024]{1,0,2:T(4,128)}) fusion(f32[4,128,1024]{1,0,2:T(4,128)S(1)} %copy-done.6, f32[4,128]{1,0:T(4,128)S(1)} %fusion.51, f32[4,128]{1,0:T(4,128)S(1)} %get-tuple-element.7, f32[1024,4,128]{2,1,0:T(4,128)} %fusion, pred[128,128]{1,0:T(8,128)(4,1)S(1)} %fusion.47, ...), kind=kOutput, calls=%fused_computation.31 | convolution fusion | flops 173015040 | bytes 45125632 | tf_op jit(solution)/shard_map/cts,bsc->btc/dot_general | solution.py:30
  281.1 7.7 %fusion.18 = bf16[512,3072]{1,0:T(8,128)(2,1)} fusion(bf16[1,1024,3072]{2,1,0:T(8,128)(2,1)} %param.11, bf16[128,8,4,128]{3,2,1,0:T(4,128)(2,1)S(1)} %bitcast.90), kind=kOutput, calls=%fused_computation.22 | convolution fusion | flops 3222798336 | bytes 10485760 | tf_op jit(solution)/shard_map/dot_general | solution.py:80
  288.8 0.0 reduce-scatter.2.cloned.1.call-update
  288.8 0.0 copy-start.9
  288.9 61.8 %reduce-scatter.2.cloned.1.call-done = bf16[128,3072]{1,0:T(8,128)(2,1)} async-done(((bf16[512,3072]{1,0:T(8,128)(2,1)}), bf16[128,3072]{1,0:T(8,128)(2,1)}) %reduce-scatter.2.cloned.1.call-update) | async-done | bytes 786448 | tf_op jit(solution)/shard_map/reduce_scatter | solution.py:79
  350.7 2.2 add_convert_fusion
  352.9 1.5 collective-permute-start.3
  354.3 1.9 copy.23
  356.3 2.2 fusion.31
  358.5 1.0 fusion.37
  359.4 12.5 %collective-permute-done.3 = bf16[128,3072]{1,0:T(8,128)(2,1)S(1)} collective-permute-done((bf16[128,3072]{1,0:T(8,128)(2,1)}, bf16[128,3072]{1,0:T(8,128)(2,1)S(1)}, u32[]{:S(2)}, u32[]{:S(2)}) %collective-permute-start.3) | collective-permute-done | bytes 786464 | tf_op jit(solution)/shard_map/ppermute | solution.py:13
  371.9 0.9 copy.39
  (25 shorter events, 0.2 us)
Async XLA Ops:
  7.2 209.4 %all-reduce.3.cloned.1.call-start = ((), (), s32[]{:S(2)}) async-start(), calls=%async_computation.1 | async-start | bytes 6291456 | tf_op jit(solution)/shard_map/psum | solution.py:74
  7.2 22.9 %collective-permute-start = (bf16[128,3072]{1,0:T(8,128)(2,1)}, bf16[128,3072]{1,0:T(8,128)(2,1)S(1)}, u32[]{:S(2)}, u32[]{:S(2)}) collective-permute-start(bf16[128,3072]{1,0:T(8,128)(2,1)} %bitcast.83), channel_id=1, source_target_pairs={{0,4},{4,8},{8,12},{12,0},{1,5},{5,9},{9,13},{13,1},{2,6},{6,10},{... | collective-permute-start | bytes 2359304 | tf_op jit(solution)/shard_map/ppermute | solution.py:58
  30.1 20.5 %collective-permute-start.1 = (bf16[128,3072]{1,0:T(8,128)(2,1)S(1)}, bf16[128,3072]{1,0:T(8,128)(2,1)S(1)}, u32[]{:S(2)}, u32[]{:S(2)}) collective-permute-start(bf16[128,3072]{1,0:T(8,128)(2,1)S(1)} %collective-permute-done), channel_id=1, source_target_pairs={{0,4},{4,8},{8,12},{12,0},{1,5},{5,9},{9,13},{13,1},{2,6},{6,10},{... | collective-permute-start | bytes 2359304 | tf_op jit(solution)/shard_map/ppermute | solution.py:58
  50.6 24.7 %collective-permute-start.2 = (bf16[128,3072]{1,0:T(8,128)(2,1)S(1)}, bf16[128,3072]{1,0:T(8,128)(2,1)S(1)}, u32[]{:S(2)}, u32[]{:S(2)}) collective-permute-start(bf16[128,3072]{1,0:T(8,128)(2,1)S(1)} %collective-permute-done.1), channel_id=1, source_target_pairs={{0,4},{4,8},{8,12},{12,0},{1,5},{5,9},{9,13},{13,1},{2,6},{6,10},{... | collective-permute-start | bytes 2359304 | tf_op jit(solution)/shard_map/ppermute | solution.py:58
  50.6 24.9 %copy-start.3 = (bf16[1,128,3072]{2,1,0:T(8,128)(2,1)S(1)}, bf16[1,128,3072]{2,1,0:T(8,128)(2,1)}, u32[]{:S(2)}) copy-start(bf16[1,128,3072]{2,1,0:T(8,128)(2,1)} %param.7) | copy-start | bytes 2359300
  75.3 3.2 copy-start.10
  75.8 2.7 copy-start.5
  78.5 16.7 %copy-start.8 = (bf16[1,1024,128]{2,1,0:T(8,128)(2,1)S(1)}, bf16[1,1024,128]{2,1,0:T(8,128)(2,1)}, u32[]{:S(2)}) copy-start(bf16[1,1024,128]{2,1,0:T(8,128)(2,1)} %param.10) | copy-start | bytes 786436
  94.5 256.2 %reduce-scatter.2.cloned.1.call-start = ((), (), s32[]{:S(2)}) async-start(), calls=%async_computation.2 | async-start | bytes 3932160 | tf_op jit(solution)/shard_map/reduce_scatter | solution.py:79
  216.6 7.8 %copy-start = (bf16[512,3,1024]{2,0,1:T(8,128)(2,1)S(1)}, bf16[512,3,1024]{2,0,1:T(8,128)(2,1)}, u32[]{:S(2)}) copy-start(bf16[512,3,1024]{2,0,1:T(8,128)(2,1)} %all-reduce.3.cloned.1.call-done) | copy-start | bytes 9437188
  225.1 2.6 copy-start.1
  228.3 4.8 %copy-start.2 = (f32[512,1,1024]{2,0,1:T(8,128)S(1)}, f32[512,1,1024]{2,0,1:T(8,128)}, u32[]{:S(2)}) copy-start(f32[512,1,1024]{2,0,1:T(8,128)} %get-tuple-element.5) | copy-start | bytes 6291460
  230.1 4.8 %copy-start.7 = (bf16[3,128,1024]{1,0,2:T(4,128)(2,1)S(1)}, bf16[3,128,1024]{1,0,2:T(4,128)(2,1)}, u32[]{:S(2)}) copy-start(bf16[3,128,1024]{1,0,2:T(4,128)(2,1)} %copy.22) | copy-start | bytes 2359300
  234.9 22.9 %copy-start.6 = (f32[4,128,1024]{1,0,2:T(4,128)S(1)}, f32[4,128,1024]{1,0,2:T(4,128)}, u32[]{:S(2)}) copy-start(f32[4,128,1024]{1,0,2:T(4,128)} %copy.17) | copy-start | bytes 6291460
  281.1 69.5 %copy-start.4 = (bf16[1,128,3072]{2,1,0:T(8,128)(2,1)S(1)}, bf16[1,128,3072]{2,1,0:T(8,128)(2,1)}, u32[]{:S(2)}) copy-start(bf16[1,128,3072]{2,1,0:T(8,128)(2,1)} %param.7) | copy-start | bytes 2359300
  288.8 69.6 %copy-start.9 = (s32[1,64]{1,0:T(1,128)S(1)}, s32[1,64]{1,0:T(1,128)}, u32[]{:S(2)}) copy-start(s32[1,64]{1,0:T(1,128)} %param.13) | copy-start | bytes 772
  352.9 19.1 %collective-permute-start.3 = (bf16[128,3072]{1,0:T(8,128)(2,1)}, bf16[128,3072]{1,0:T(8,128)(2,1)S(1)}, u32[]{:S(2)}, u32[]{:S(2)}) collective-permute-start(bf16[128,3072]{1,0:T(8,128)(2,1)} %add_convert_fusion), channel_id=1, source_target_pairs={{0,2},{2,0},{1,3},{3,1},{4,6},{6,4},{5,7},{7,5},{8,10},{10,8},{9,1... | collective-permute-start | bytes 2359304 | tf_op jit(solution)/shard_map/ppermute | solution.py:13
Sparse Core Ops, SparseCore 0:
  94.6 24.5 all-reduce.2
  289.0 61.6 reduce-scatter.1
